TPU v7x, 32 devices: a whole 2x2x4 slice. The times are simulated.
32 devices in a mesh: groups: 2 (over y), ctx: 4 (over z), exp: 2 (over x), tp: 2 (over core).
Axes of the slice: x: 2, y: 2, z: 4, core: 2. Of those that a mesh axis runs over, the one named last changes fastest.
Arguments:
- queries: bfloat16 [4, 512, 20, 128], P(('groups', 'exp'), 'ctx', 'tp'), parts along dimension 0, may hold values from -9 to 9
- key_states: bfloat16 [4, 512, 4, 128], P(('groups', 'exp'), 'ctx', 'tp'), parts along dimension 0, may hold values from -9 to 9
- values: bfloat16 [4, 512, 4, 128], P(('groups', 'exp'), 'ctx', 'tp'), parts along dimension 0, may hold values from -6 to 6
- doc_ids: int32 [4, 512], P(('groups', 'exp'), 'ctx'), parts along dimension 0, may hold values from 0 to 3, never falling along the last dimension, each value on 1 to 256 neighbouring positions
- residual: bfloat16 [4, 512, 5120], P(('groups', 'exp'), ('ctx', 'tp')), parts along dimension 0, may hold values from -6 to 6
- out_proj: bfloat16 [2560, 5120], P('tp', 'ctx'), may hold values from -0.125 to 0.125
- norm_gain: bfloat16 [5120], replicated, may hold values from 0.5 to 1.5
- router: bfloat16 [5120, 64], P(None, 'exp'), may hold values from -0.078125 to 0.078125
- expert_ids: int32 [4, 512, 1], P(('groups', 'exp'), ('ctx', 'tp')), parts along dimension 0, may hold values from 0 to 63; in each aligned block of 64 rows (0 to 63, 64 to 127, ..., all dimensions but the last counted through in order) at most 2 rows name the same one
- keep_counts: int32 [128], P('groups'), parts along dimension 0, may hold values from 1 to 2
Outputs:
- expert_inputs: bfloat16 [32, 64, 2, 5120], P(('groups', 'ctx', 'tp'), 'exp'), parts along dimension 0
There are 2 independent parts, one for each index of `groups`. A program takes and returns all parts, laid end to end along the dimension named above; an argument that names none is the same for every part. Nothing has to cross between parts.
Inputs may be any that keep to these rules, and one draw needn't show every extreme that they name: `doc_ids`: doc ids never fall along a request; a document holds at most 256 tokens, and some document holds exactly that many. `expert_ids`: in each aligned block of 64 tokens (the rows of one device) no expert is named more than 2 times, and in some blocks one expert is named exactly 2 times.
All inputs are finite; a program needn't handle non-finite values.
Results may differ from a plain program's by a relative error of at most 0.013.
Values may be sent and summed in bfloat16 or wider, within the bound.
A program may use at most 64 MiB of HBM per device.

v0:
```python
import math
import jax
import jax.numpy as jnp
from jax import lax
from jax.sharding import PartitionSpec as P

CAP = 2
EPSILON = 1e-05


def on_device(
    queries,
    key_states,
    values,
    doc_ids,
    residual,
    out_proj,
    norm_gain,
    router,
    expert_ids,
    keep_counts,
):
    tokens_here = queries.shape[1]
    heads_here = queries.shape[2]
    head_size = queries.shape[3]
    groups_here = key_states.shape[2]
    mixing_ratio = heads_here // groups_here
    ctx_count = lax.axis_size("ctx")
    pair_count = lax.axis_size("tp")
    part_rows = tokens_here // pair_count
    first_token = lax.axis_index("ctx") * tokens_here
    scale = 1.0 / math.sqrt(head_size)
    query_rows = (
        queries[0].reshape(tokens_here, groups_here, mixing_ratio, head_size).transpose(1, 0, 2, 3)
    )
    query_rows = query_rows.reshape(groups_here, tokens_here * mixing_ratio, head_size)
    query_place = (
        first_token
        + lax.broadcasted_iota(jnp.int32, (tokens_here * mixing_ratio,), 0) // mixing_ratio
    )
    query_docs = jnp.repeat(doc_ids[0], mixing_ratio)

    def update(running, key_block, value_block, doc_block, key_first):
        highest, totals, accum = running
        scores = (
            jnp.einsum("gqd,kgd->gqk", query_rows, key_block, preferred_element_type=jnp.float32)
            * scale
        )
        key_place = key_first + lax.broadcasted_iota(jnp.int32, (key_block.shape[0],), 0)
        allowed = (key_place[None, :] <= query_place[:, None]) & (
            doc_block[None, :] == query_docs[:, None]
        )
        masked = jnp.where(allowed[None], scores, -1e30)
        new_highest = jnp.maximum(highest, jnp.max(masked, axis=2))
        weights = jnp.where(allowed[None], jnp.exp(scores - new_highest[..., None]), 0.0)
        factor = jnp.exp(highest - new_highest)
        totals = totals * factor + jnp.sum(weights, axis=2)
        accum = accum * factor[..., None] + jnp.einsum(
            "gqk,kgd->gqd",
            weights.astype(jnp.bfloat16),
            value_block,
            preferred_element_type=jnp.float32,
        )
        return (new_highest, totals, accum)

    start_state = (
        jnp.full((groups_here, tokens_here * mixing_ratio), -1e30, jnp.float32),
        jnp.zeros((groups_here, tokens_here * mixing_ratio), jnp.float32),
        jnp.zeros((groups_here, tokens_here * mixing_ratio, head_size), jnp.float32),
    )
    key_piece = lax.all_gather(key_states, "ctx", axis=1, tiled=True)
    value_piece = lax.all_gather(values, "ctx", axis=1, tiled=True)
    doc_piece = lax.all_gather(doc_ids, "ctx", axis=1, tiled=True)
    piece_rows = key_piece.shape[1]
    block_rows = math.gcd(piece_rows, 512)

    def step(block_number, inner):
        block_offset = block_number * block_rows
        key_block = lax.dynamic_slice_in_dim(key_piece[0], block_offset, block_rows, 0)
        value_block = lax.dynamic_slice_in_dim(value_piece[0], block_offset, block_rows, 0)
        doc_block = lax.dynamic_slice_in_dim(doc_piece[0], block_offset, block_rows, 0)
        return update(inner, key_block, value_block, doc_block, block_offset)

    highest, totals, accum = lax.fori_loop(0, piece_rows // block_rows, step, start_state)
    blended_output = (accum / totals[..., None]).astype(jnp.bfloat16)
    blended_output = blended_output.reshape(
        groups_here, tokens_here, mixing_ratio, head_size
    ).transpose(1, 0, 2, 3)
    attn_rows = blended_output.reshape(pair_count, part_rows, heads_here * head_size)
    columns = out_proj.shape[1]
    gathered = lax.all_gather(attn_rows, "ctx", axis=1, tiled=True)
    gathered = gathered.reshape(pair_count * ctx_count * part_rows, heads_here * head_size)
    own_columns = lax.psum_scatter(
        jnp.dot(gathered, out_proj, preferred_element_type=jnp.float32).astype(jnp.bfloat16),
        "tp",
        scatter_dimension=0,
        tiled=True,
    ).astype(jnp.float32)
    own_columns = own_columns.reshape(ctx_count, part_rows, columns)
    projected = (
        lax.all_to_all(
            own_columns.astype(jnp.bfloat16), "ctx", split_axis=0, concat_axis=2, tiled=True
        )
        .astype(own_columns.dtype)
        .reshape(part_rows, columns * ctx_count)
    )
    hidden = residual[0].astype(jnp.float32) + projected
    power = jnp.mean(hidden * hidden, axis=1, keepdims=True)
    normed = (hidden * lax.rsqrt(power + EPSILON) * norm_gain.astype(jnp.float32)).astype(
        jnp.bfloat16
    )
    expert_count = keep_counts.shape[0]
    chosen = expert_ids[0, :, 0]
    onehot = (
        chosen[:, None] == lax.broadcasted_iota(jnp.int32, (part_rows, expert_count), 1)
    ).astype(jnp.float32)
    lower = (
        lax.broadcasted_iota(jnp.int32, (part_rows, part_rows), 0)
        > lax.broadcasted_iota(jnp.int32, (part_rows, part_rows), 1)
    ).astype(jnp.float32)
    earlier = jnp.dot(lower, onehot, preferred_element_type=jnp.float32)
    ranking = jnp.sum(onehot * earlier, axis=1)
    limits = jnp.sum(onehot * keep_counts.astype(jnp.float32)[None, :], axis=1)
    kept = ranking < limits
    target = chosen.astype(jnp.float32) * CAP + ranking
    slot_iota = lax.broadcasted_iota(jnp.int32, (expert_count * CAP, part_rows), 0).astype(
        jnp.float32
    )
    table = (slot_iota == target[None, :]) & kept[None, :]
    outgoing = jnp.dot(
        table.astype(jnp.bfloat16), normed, preferred_element_type=jnp.float32
    ).astype(jnp.bfloat16)
    exp_count = lax.axis_size("exp")
    outgoing = outgoing.reshape(exp_count, expert_count // exp_count, CAP, normed.shape[1])
    arrived = lax.all_to_all(outgoing, "exp", split_axis=0, concat_axis=0, tiled=True)
    logits = jnp.einsum("secd,de->sec", arrived, router, preferred_element_type=jnp.float32)
    return (arrived.astype(jnp.float32) * jax.nn.sigmoid(logits)[..., None]).astype(jnp.bfloat16)


def solution(mesh):
    placed = (
        P(("groups", "exp"), "ctx", "tp", None),
        P(("groups", "exp"), "ctx", "tp", None),
        P(("groups", "exp"), "ctx", "tp", None),
        P(("groups", "exp"), "ctx"),
        P(("groups", "exp"), ("ctx", "tp"), None),
        P("tp", "ctx"),
        P(),
        P(None, "exp"),
        P(("groups", "exp"), ("ctx", "tp"), None),
        P("groups"),
    )
    return jax.shard_map(
        on_device,
        mesh=mesh,
        in_specs=placed,
        out_specs=P(("groups", "ctx", "tp"), "exp", None, None),
        check_vma=False,
    )
```

profile of v0, /device:TPU:0, one launch (start us, length us, event | category | flops | bytes accessed | tf_op | source)
XLA Modules:
  0.0 172.3 jit_solution(3476322581073212627)
XLA Ops:
  6.5 0.0 copy-start
  6.5 0.0 all-gather.2.cloned.1.call-start
  6.5 12.9 %all_gather.14 = s32[1,512]{1,0:T(1,128)S(1)} all-gather(s32[1,128]{1,0:T(1,128)} %param.13), channel_id=1, replica_groups=mesh['groups'=2,'ctx'=4,'exp'=2,'tp'=2] {'ctx'}, dimensions={1}, use_global_device_ids=true | all-gather | bytes 2560 | tf_op jit(solution)/shard_map/all_gather | solution.py:73
  19.5 0.7 broadcast_in_dim.55
  20.2 0.2 eq.47
  20.4 0.9 copy.17
  21.3 13.9 %all_gather.16 = bf16[1,512,2,128]{3,1,2,0:T(8,128)(2,1)S(1)} all-gather(bf16[1,128,2,128]{3,1,2,0:T(8,128)(2,1)S(1)} %copy.17), channel_id=1, replica_groups=mesh['groups'=2,'ctx'=4,'exp'=2,'tp'=2] {'ctx'}, dimensions={1}, use_global_device_ids=true | all-gather | bytes 327680 | tf_op jit(solution)/shard_map/all_gather | solution.py:71
  35.2 1.3 copy.16
  36.5 0.3 fusion.7
  36.8 0.7 select_reduce_fusion
  37.5 0.0 copy-start.2
  37.5 0.6 fusion
  38.1 0.2 copy-done.2
  38.3 14.1 %all_gather.17 = bf16[1,512,2,128]{3,1,2,0:T(8,128)(2,1)S(1)} all-gather(bf16[1,128,2,128]{3,1,2,0:T(8,128)(2,1)S(1)} %copy.19), channel_id=1, replica_groups=mesh['groups'=2,'ctx'=4,'exp'=2,'tp'=2] {'ctx'}, dimensions={1}, use_global_device_ids=true | all-gather | bytes 327680 | tf_op jit(solution)/shard_map/all_gather | solution.py:72
  52.5 1.2 fusion.18
  53.7 0.3 copy.21
  54.0 0.9 copy.22
  54.9 2.2 %reshape.135 = bf16[2,64,1280]{2,1,0:T(8,128)(2,1)} reshape(bf16[128,2,5,128]{3,2,1,0:T(8,128)(2,1)} %copy.22) | data formatting | bytes 655360 | tf_op jit(solution)/shard_map/reshape | solution.py:89
  57.1 0.0 all-gather.2.cloned.1.call-update
  57.1 0.0 reduce-scatter.2.cloned.1.call-start
  57.1 30.9 %all-gather.2.cloned.1.call-done = bf16[2,256,1280]{2,1,0:T(8,128)(2,1)} async-done(((bf16[2,64,1280]{2,1,0:T(8,128)(2,1)}), bf16[2,256,1280]{2,1,0:T(8,128)(2,1)}) %all-gather.2.cloned.1.call-update) | async-done | bytes 1310736 | tf_op jit(solution)/shard_map/all_gather | solution.py:91
  88.1 0.0 copy-done
  88.1 4.2 %convolution_convert_fusion.1 = bf16[512,1280]{1,0:T(8,128)(2,1)} fusion(bf16[512,1280]{1,0:T(8,128)(2,1)} %bitcast.62, bf16[1280,1280]{1,0:T(8,128)(2,1)S(1)} %copy-done), kind=kOutput, calls=%fused_computation.1 | convolution fusion | flops 1678376960 | bytes 5898240 | tf_op jit(solution)/shard_map/dot_general | solution.py:94
  92.3 0.0 copy-start.6
  92.3 0.0 copy-start.3
  92.3 0.0 copy-start.4
  92.3 0.0 reduce-scatter.2.cloned.1.call-update
  92.3 7.9 %reduce-scatter.2.cloned.1.call-done = bf16[256,1280]{1,0:T(8,128)(2,1)} async-done(((bf16[512,1280]{1,0:T(8,128)(2,1)}), bf16[256,1280]{1,0:T(8,128)(2,1)}) %reduce-scatter.2.cloned.1.call-update) | async-done | bytes 655376 | tf_op jit(solution)/shard_map/reduce_scatter | solution.py:93
  100.3 5.0 %all-to-all-start = ((bf16[4,64,1280]{2,1,0:T(8,128)(2,1)}), bf16[4,64,1280]{2,1,0:T(8,128)(2,1)}, u32[]{:S(2)}, u32[]{:S(2)}) async-start(bf16[4,64,1280]{2,1,0:T(8,128)(2,1)} %bitcast.55), calls=%async_computation.1 | async-start | bytes 1310720 | tf_op jit(solution)/shard_map/all_to_all | solution.py:101
  105.3 0.0 copy-done.6
  105.3 0.0 copy-done.3
  105.3 0.0 copy-done.4
  105.3 0.2 fusion.14
  105.4 0.1 select_reduce_fusion.1
  105.6 17.4 %all-to-all-done = bf16[4,64,1280]{2,1,0:T(8,128)(2,1)} async-done(((bf16[4,64,1280]{2,1,0:T(8,128)(2,1)}), bf16[4,64,1280]{2,1,0:T(8,128)(2,1)}, u32[]{:S(2)}, u32[]{:S(2)}) %all-to-all-start) | async-done | bytes 655392 | tf_op jit(solution)/shard_map/all_to_all | solution.py:101
  123.0 1.2 convert_bitcast_fusion
  124.2 0.8 copy.23
  125.0 0.0 copy-start.1
  125.0 0.2 copy.28
  125.3 0.8 copy-done.1
  126.1 0.3 multiply_reduce_fusion
  126.4 1.6 convolution_convert_fusion
  128.0 3.9 %reshape.137 = bf16[2,32,2,5120]{3,2,1,0:T(2,128)(2,1)} reshape(bf16[128,5120]{1,0:T(8,128)(2,1)} %convolution_convert_fusion) | data formatting | bytes 2621440 | tf_op jit(solution)/shard_map/reshape | solution.py:134
  131.9 0.0 copy-start.5
  131.9 19.7 %all_to_all.14 = bf16[2,32,2,5120]{3,2,1,0:T(2,128)(2,1)S(1)} all-to-all(bf16[2,32,2,5120]{3,2,1,0:T(2,128)(2,1)} %reshape.137), channel_id=1, replica_groups=mesh['groups'=2,'ctx'=4,'exp'=2,'tp'=2] {'exp'}, dimensions={0} | all-to-all | bytes 2621440 | tf_op jit(solution)/shard_map/all_to_all | solution.py:135
  151.6 0.0 copy-done.5
  151.6 11.5 %fusion.9 = f32[32,1,2,2]{3,1,2,0:T(1,128)S(1)} fusion(bf16[2,32,2,5120]{3,2,1,0:T(2,128)(2,1)S(1)} %all_to_all.14, bf16[5120,32,1,1]{0,1,2,3:T(8,128)(2,1)S(1)} %bitcast.63), kind=kOutput, calls=%fused_computation.18 | convolution fusion | flops 1310720 | bytes 1638912 | tf_op jit(solution)/shard_map/secd,de->sec/dot_general | solution.py:136
  163.2 2.2 %multiply_convert_fusion = bf16[2,32,2,5120]{3,2,1,0:T(2,128)(2,1)} fusion(bf16[2,32,2,5120]{3,2,1,0:T(2,128)(2,1)S(1)} %all_to_all.14, f32[2,32,2]{2,1,0:T(8,128)S(1)} %fusion.34), kind=kLoop, calls=%fused_computation.2 | loop fusion | flops 1966080 | bytes 2621952 | tf_op jit(solution)/shard_map/convert_element_type | solution.py:137
  (10 shorter events, 0.1 us)
Async XLA Ops:
  6.5 81.5 %copy-start = (bf16[1280,1280]{1,0:T(8,128)(2,1)S(1)}, bf16[1280,1280]{1,0:T(8,128)(2,1)}, u32[]{:S(2)}) copy-start(bf16[1280,1280]{1,0:T(8,128)(2,1)} %param.15) | copy-start | bytes 9830404
  6.5 81.5 %all-gather.2.cloned.1.call-start = ((), (), s32[]{:S(2)}) async-start(), calls=%async_computation.3 | async-start | bytes 1638400 | tf_op jit(solution)/shard_map/all_gather | solution.py:91
  37.5 0.8 copy-start.2
  57.1 43.2 %reduce-scatter.2.cloned.1.call-start = ((), (), s32[]{:S(2)}) async-start(), calls=%async_computation.4 | async-start | bytes 1966080 | tf_op jit(solution)/shard_map/reduce_scatter | solution.py:93
  92.3 13.0 %copy-start.6 = (s32[64]{0:T(128)S(1)}, s32[64]{0:T(128)}, u32[]{:S(2)}) copy-start(s32[64]{0:T(128)} %param.19) | copy-start | bytes 772
  92.3 13.0 %copy-start.3 = (bf16[5120]{0:T(1024)(128)(2,1)S(1)}, bf16[5120]{0:T(1024)(128)(2,1)}, u32[]{:S(2)}) copy-start(bf16[5120]{0:T(1024)(128)(2,1)} %param.16) | copy-start | bytes 30724
  92.3 13.0 %copy-start.4 = (s32[1,64,1]{1,2,0:T(1,128)S(1)}, s32[1,64,1]{1,2,0:T(1,128)}, u32[]{:S(2)}) copy-start(s32[1,64,1]{1,2,0:T(1,128)} %param.18) | copy-start | bytes 772
  100.3 22.7 %all-to-all-start = ((bf16[4,64,1280]{2,1,0:T(8,128)(2,1)}), bf16[4,64,1280]{2,1,0:T(8,128)(2,1)}, u32[]{:S(2)}, u32[]{:S(2)}) async-start(bf16[4,64,1280]{2,1,0:T(8,128)(2,1)} %bitcast.55), calls=%async_computation.1 | async-start | bytes 1310720 | tf_op jit(solution)/shard_map/all_to_all | solution.py:101
  125.0 1.1 copy-start.1
  131.9 19.7 %copy-start.5 = (bf16[5120,32]{0,1:T(8,128)(2,1)S(1)}, bf16[5120,32]{0,1:T(8,128)(2,1)}, u32[]{:S(2)}) copy-start(bf16[5120,32]{0,1:T(8,128)(2,1)} %param.17) | copy-start | bytes 983044
Sparse Core Ops, SparseCore 0:
  57.2 30.8 all-gather.1
  92.4 7.7 reduce-scatter.1
where the time goes:
time: 173 us; the launch traced here: 172 us
  blocking collectives  60.6 us (35%)
  waiting for transfers between devices  56.3 us (33%)
  matrix products  19.5 us (11%)
  between operations  13.6 us (8%)
  local copies, waits for them, and re-layouts  12.5 us (7%)
  starting transfers between devices  5.02 us (3%)
  other arithmetic  4.83 us (3%)
    all_gather x1, waiting for transfers between devices, on_device(): gathered = lax.all_gather(attn_rows, 'ctx', axis=1, tiled=True)  30.9 us
    all_to_all x1, blocking collectives, on_device(): lax.all_to_all(outgoing, 'exp', split_axis=0, concat_axis=0, tiled=True)  19.7 us
    all_to_all x1, waiting for transfers between devices, on_device(): lax.all_to_all(own_columns.astype(jnp.bfloat16), 'ctx', split_axis=0, con...  17.4 us
    all_gather x1, blocking collectives, on_device(): value_piece = lax.all_gather(values, 'ctx', axis=1, tiled=True)  14.1 us
    all_gather x1, blocking collectives, on_device(): key_piece = lax.all_gather(key_states, 'ctx', axis=1, tiled=True)  13.9 us
    all_gather x1, blocking collectives, on_device(): doc_piece = lax.all_gather(doc_ids, 'ctx', axis=1, tiled=True)  12.9 us
    dot_general x1, matrix products, on_device(): jnp.einsum('secd,de->sec', arrived, router, preferred_element_type=jnp.fl...  11.5 us
    reduce_scatter x1, waiting for transfers between devices, on_device(): lax.psum_scatter(jnp.dot(gathered, out_proj, preferred_element_type=jnp.f...  7.95 us
  transfers between devices with their start and end apart: 3, of which 3 were waited for; matrix products, arithmetic and copies ran while one was open for 0% of the time, Pallas kernels for 0%

commit v1 on v0

--- a/solution.py
+++ b/solution.py
@@ -68,7 +68,12 @@
         jnp.zeros((groups_here, tokens_here * mixing_ratio), jnp.float32),
         jnp.zeros((groups_here, tokens_here * mixing_ratio, head_size), jnp.float32),
     )
-    key_piece = lax.all_gather(key_states, "ctx", axis=1, tiled=True)
+    ring = [key_states]
+    for hop in range(3):
+        ring.append(lax.ppermute(ring[-1], "ctx", [(dev, (dev + 1) % 4) for dev in range(4)]))
+    key_piece = jnp.roll(
+        jnp.concatenate(ring[::-1], axis=1), (lax.axis_index("ctx") + 1) * ring[0].shape[1], axis=1
+    )
     value_piece = lax.all_gather(values, "ctx", axis=1, tiled=True)
     doc_piece = lax.all_gather(doc_ids, "ctx", axis=1, tiled=True)
     piece_rows = key_piece.shape[1]

time: 173 us -> 166 us (0.960)
  blocking collectives: 60.6 us -> 44 us
  waiting for transfers between devices: 56.3 us -> 61.4 us
  starting transfers between devices: 5.02 us -> 8.16 us
    all_gather x1 -> x0, blocking collectives: 13.9 us -> none  [on_device(): key_piece = lax.all_gather(key_states, 'ctx', axis=1, tiled=True)]
    ppermute x0 -> x3, starting transfers between devices: none -> 3.14 us  [on_device(): lax.ppermute(ring[-1], 'ctx', [(dev, (dev + 1) % 4) for dev in range(4)])]
    all_gather x1, waiting for transfers between devices: 30.9 us -> 33.9 us  [on_device(): gathered = lax.all_gather(attn_rows, 'ctx', axis=1, tiled=True)]
    all_gather x1, blocking collectives: 12.9 us -> 9.89 us  [on_device(): doc_piece = lax.all_gather(doc_ids, 'ctx', axis=1, tiled=True)]
    ppermute x0 -> x3, waiting for transfers between devices: none -> 2.07 us  [on_device(): lax.ppermute(ring[-1], 'ctx', [(dev, (dev + 1) % 4) for dev in range(4)])]
  transfers between devices with their start and end apart: 3 -> 6, of which waited for: 3 -> 4; matrix products, arithmetic and copies ran while one was open for 0% -> 3% of each run, Pallas kernels for 0% -> 0%
where the time goes in v1:
time: 166 us
  waiting for transfers between devices  61.4 us (37%)
  blocking collectives  44 us (27%)
  matrix products  19.5 us (12%)
  local copies, waits for them, and re-layouts  13.6 us (8%)
  between operations  13.6 us (8%)
  starting transfers between devices  8.16 us (5%)
  other arithmetic  5.56 us (3%)
    all_gather x1, waiting for transfers between devices, on_device(): gathered = lax.all_gather(attn_rows, 'ctx', axis=1, tiled=True)  33.9 us
    all_to_all x1, blocking collectives, on_device(): lax.all_to_all(outgoing, 'exp', split_axis=0, concat_axis=0, tiled=True)  19.7 us
    all_to_all x1, waiting for transfers between devices, on_device(): lax.all_to_all(own_columns.astype(jnp.bfloat16), 'ctx', split_axis=0, con...  17.4 us
    all_gather x1, blocking collectives, on_device(): value_piece = lax.all_gather(values, 'ctx', axis=1, tiled=True)  14.4 us
    dot_general x1, matrix products, on_device(): jnp.einsum('secd,de->sec', arrived, router, preferred_element_type=jnp.fl...  11.5 us
    all_gather x1, blocking collectives, on_device(): doc_piece = lax.all_gather(doc_ids, 'ctx', axis=1, tiled=True)  9.89 us
    reduce_scatter x1, waiting for transfers between devices, on_device(): lax.psum_scatter(jnp.dot(gathered, out_proj, preferred_element_type=jnp.f...  7.95 us
    all_to_all x1, starting transfers between devices, on_device(): lax.all_to_all(own_columns.astype(jnp.bfloat16), 'ctx', split_axis=0, con...  4.98 us
  transfers between devices with their start and end apart: 6, of which 4 were waited for; matrix products, arithmetic and copies ran while one was open for 3% of the time, Pallas kernels for 0%

profile of v1, /device:TPU:0, one launch (start us, length us, event | category | flops | bytes accessed | tf_op | source)
XLA Modules:
  0.0 165.8 jit_solution(3278054453467832915)
XLA Ops:
  6.5 0.0 copy-start
  6.5 0.0 copy-start.4
  6.5 0.0 all-gather.2.cloned.1.call-start
  6.5 3.1 %collective-permute-start = (bf16[1,128,2,128]{3,2,1,0:T(2,128)(2,1)}, bf16[1,128,2,128]{3,2,1,0:T(2,128)(2,1)S(1)}, u32[]{:S(2)}, u32[]{:S(2)}) collective-permute-start(bf16[1,128,2,128]{3,2,1,0:T(2,128)(2,1)} %param.11), channel_id=1, source_target_pairs={{0,4},{4,8},{8,12},{12,0},{1,5},{5,9},{9,13},{13,1},{2,6},{6,10},{... | collective-permute-start | bytes 196616 | tf_op jit(solution)/shard_map/ppermute | solution.py:73
  9.6 9.9 %all_gather.11 = s32[1,512]{1,0:T(1,128)S(1)} all-gather(s32[1,128]{1,0:T(1,128)} %param.13), channel_id=1, replica_groups=mesh['groups'=2,'ctx'=4,'exp'=2,'tp'=2] {'ctx'}, dimensions={1}, use_global_device_ids=true | all-gather | bytes 2560 | tf_op jit(solution)/shard_map/all_gather | solution.py:78
  19.5 0.7 broadcast_in_dim.55
  20.2 0.2 eq.50
  20.5 0.0 collective-permute-done
  20.5 0.1 collective-permute-start.1
  20.6 1.1 fusion.10
  21.6 2.0 %copy.17 = bf16[128,2,5,128]{3,1,2,0:T(2,128)(2,1)} copy(bf16[128,2,5,128]{3,0,2,1:T(8,128)(2,1)} %bitcast.76) | data formatting | bytes 655360 | tf_op jit(solution)/shard_map/reshape;squeeze | solution.py:34
  23.6 0.8 copy.19
  24.5 0.0 copy-start.2
  24.5 0.0 copy-start.3
  24.5 2.1 %collective-permute-done.1 = bf16[1,128,2,128]{3,2,1,0:T(2,128)(2,1)S(1)} collective-permute-done((bf16[1,128,2,128]{3,2,1,0:T(2,128)(2,1)S(1)}, bf16[1,128,2,128]{3,2,1,0:T(2,128)(2,1)S(1)}, u32[]{:S(2)}, u32[]{:S(2)}) %collective-permute-start.1) | collective-permute-done | bytes 65568 | tf_op jit(solution)/shard_map/ppermute | solution.py:73
  26.6 0.0 collective-permute-start.2
  26.6 14.4 %all_gather.13 = bf16[1,512,2,128]{3,1,2,0:T(8,128)(2,1)S(1)} all-gather(bf16[1,128,2,128]{3,1,2,0:T(8,128)(2,1)S(1)} %copy.19), channel_id=1, replica_groups=mesh['groups'=2,'ctx'=4,'exp'=2,'tp'=2] {'ctx'}, dimensions={1}, use_global_device_ids=true | all-gather | bytes 327680 | tf_op jit(solution)/shard_map/all_gather | solution.py:77
  40.9 0.0 collective-permute-done.2
  41.0 0.1 constant_dynamic-update-slice_fusion.6
  41.1 0.1 constant_dynamic-update-slice_fusion.5
  41.1 0.0 copy-done.4
  41.1 0.1 constant_dynamic-update-slice_fusion.4
  41.2 0.1 constant_dynamic-update-slice_fusion.3
  41.3 0.1 constant_dynamic-update-slice_fusion.2
  41.3 0.1 constant_dynamic-update-slice_fusion.1
  41.4 0.1 constant_dynamic-update-slice_fusion
  41.4 0.2 constant_dynamic-slice_fusion
  41.6 0.0 copy-done.2
  41.6 0.0 copy-done.3
  41.7 0.7 fusion
  42.4 0.6 fusion.3
  43.0 1.2 fusion.21
  44.2 0.3 copy.21
  44.6 0.9 copy.22
  45.5 2.1 %reshape.135 = bf16[2,64,1280]{2,1,0:T(8,128)(2,1)} reshape(bf16[128,2,5,128]{3,2,1,0:T(8,128)(2,1)} %copy.22) | data formatting | bytes 655360 | tf_op jit(solution)/shard_map/reshape | solution.py:94
  47.6 0.0 all-gather.2.cloned.1.call-update
  47.6 0.0 reduce-scatter.2.cloned.1.call-start
  47.7 33.9 %all-gather.2.cloned.1.call-done = bf16[2,256,1280]{2,1,0:T(8,128)(2,1)} async-done(((bf16[2,64,1280]{2,1,0:T(8,128)(2,1)}), bf16[2,256,1280]{2,1,0:T(8,128)(2,1)}) %all-gather.2.cloned.1.call-update) | async-done | bytes 1310736 | tf_op jit(solution)/shard_map/all_gather | solution.py:96
  81.6 0.0 copy-done
  81.6 4.2 %convolution_convert_fusion.1 = bf16[512,1280]{1,0:T(8,128)(2,1)} fusion(bf16[512,1280]{1,0:T(8,128)(2,1)} %bitcast.82, bf16[1280,1280]{1,0:T(8,128)(2,1)S(1)} %copy-done), kind=kOutput, calls=%fused_computation.1 | convolution fusion | flops 1678376960 | bytes 5898240 | tf_op jit(solution)/shard_map/dot_general | solution.py:99
  85.9 0.0 copy-start.8
  85.9 0.0 copy-start.5
  85.9 0.0 copy-start.6
  85.9 0.0 reduce-scatter.2.cloned.1.call-update
  85.9 7.9 %reduce-scatter.2.cloned.1.call-done = bf16[256,1280]{1,0:T(8,128)(2,1)} async-done(((bf16[512,1280]{1,0:T(8,128)(2,1)}), bf16[256,1280]{1,0:T(8,128)(2,1)}) %reduce-scatter.2.cloned.1.call-update) | async-done | bytes 655376 | tf_op jit(solution)/shard_map/reduce_scatter | solution.py:98
  93.8 5.0 %all-to-all-start = ((bf16[4,64,1280]{2,1,0:T(8,128)(2,1)}), bf16[4,64,1280]{2,1,0:T(8,128)(2,1)}, u32[]{:S(2)}, u32[]{:S(2)}) async-start(bf16[4,64,1280]{2,1,0:T(8,128)(2,1)} %bitcast.75), calls=%async_computation.1 | async-start | bytes 1310720 | tf_op jit(solution)/shard_map/all_to_all | solution.py:106
  98.8 0.0 copy-done.8
  98.8 0.0 copy-done.5
  98.8 0.0 copy-done.6
  98.8 0.2 fusion.17
  99.0 0.1 select_reduce_fusion
  99.1 17.4 %all-to-all-done = bf16[4,64,1280]{2,1,0:T(8,128)(2,1)} async-done(((bf16[4,64,1280]{2,1,0:T(8,128)(2,1)}), bf16[4,64,1280]{2,1,0:T(8,128)(2,1)}, u32[]{:S(2)}, u32[]{:S(2)}) %all-to-all-start) | async-done | bytes 655392 | tf_op jit(solution)/shard_map/all_to_all | solution.py:106
  116.5 1.2 convert_bitcast_fusion
  117.7 0.8 copy.23
  118.6 0.0 copy-start.1
  118.6 0.2 copy.28
  118.8 0.8 copy-done.1
  119.7 0.3 multiply_reduce_fusion
  120.0 1.6 convolution_convert_fusion
  121.6 3.8 %reshape.137 = bf16[2,32,2,5120]{3,2,1,0:T(2,128)(2,1)} reshape(bf16[128,5120]{1,0:T(8,128)(2,1)} %convolution_convert_fusion) | data formatting | bytes 2621440 | tf_op jit(solution)/shard_map/reshape | solution.py:139
  125.4 19.7 %all_to_all.14 = bf16[2,32,2,5120]{3,2,1,0:T(2,128)(2,1)S(1)} all-to-all(bf16[2,32,2,5120]{3,2,1,0:T(2,128)(2,1)} %reshape.137), channel_id=1, replica_groups=mesh['groups'=2,'ctx'=4,'exp'=2,'tp'=2] {'exp'}, dimensions={0} | all-to-all | bytes 2621440 | tf_op jit(solution)/shard_map/all_to_all | solution.py:140
  145.1 0.0 copy-done.7
  145.1 11.5 %fusion.12 = f32[32,1,2,2]{3,1,2,0:T(1,128)S(1)} fusion(bf16[2,32,2,5120]{3,2,1,0:T(2,128)(2,1)S(1)} %all_to_all.14, bf16[5120,32,1,1]{0,1,2,3:T(8,128)(2,1)S(1)} %bitcast.83), kind=kOutput, calls=%fused_computation.21 | convolution fusion | flops 1310720 | bytes 1638912 | tf_op jit(solution)/shard_map/secd,de->sec/dot_general | solution.py:141
  156.8 2.2 %multiply_convert_fusion = bf16[2,32,2,5120]{3,2,1,0:T(2,128)(2,1)} fusion(bf16[2,32,2,5120]{3,2,1,0:T(2,128)(2,1)S(1)} %all_to_all.14, f32[2,32,2]{2,1,0:T(8,128)S(1)} %fusion.38), kind=kLoop, calls=%fused_computation.7 | loop fusion | flops 1966080 | bytes 2621952 | tf_op jit(solution)/shard_map/convert_element_type | solution.py:142
  (11 shorter events, 0.2 us)
Async XLA Ops:
  6.5 75.1 %copy-start = (bf16[1280,1280]{1,0:T(8,128)(2,1)S(1)}, bf16[1280,1280]{1,0:T(8,128)(2,1)}, u32[]{:S(2)}) copy-start(bf16[1280,1280]{1,0:T(8,128)(2,1)} %param.15) | copy-start | bytes 9830404
  6.5 34.6 %copy-start.4 = (bf16[1,128,2,128]{3,2,1,0:T(2,128)(2,1)S(1)}, bf16[1,128,2,128]{3,2,1,0:T(2,128)(2,1)}, u32[]{:S(2)}) copy-start(bf16[1,128,2,128]{3,2,1,0:T(2,128)(2,1)} %param.11) | copy-start | bytes 196612
  6.5 75.1 %all-gather.2.cloned.1.call-start = ((), (), s32[]{:S(2)}) async-start(), calls=%async_computation.3 | async-start | bytes 1638400 | tf_op jit(solution)/shard_map/all_gather | solution.py:96
  6.5 13.9 %collective-permute-start = (bf16[1,128,2,128]{3,2,1,0:T(2,128)(2,1)}, bf16[1,128,2,128]{3,2,1,0:T(2,128)(2,1)S(1)}, u32[]{:S(2)}, u32[]{:S(2)}) collective-permute-start(bf16[1,128,2,128]{3,2,1,0:T(2,128)(2,1)} %param.11), channel_id=1, source_target_pairs={{0,4},{4,8},{8,12},{12,0},{1,5},{5,9},{9,13},{13,1},{2,6},{6,10},{... | collective-permute-start | bytes 196616 | tf_op jit(solution)/shard_map/ppermute | solution.py:73
  20.5 6.1 %collective-permute-start.1 = (bf16[1,128,2,128]{3,2,1,0:T(2,128)(2,1)S(1)}, bf16[1,128,2,128]{3,2,1,0:T(2,128)(2,1)S(1)}, u32[]{:S(2)}, u32[]{:S(2)}) collective-permute-start(bf16[1,128,2,128]{3,2,1,0:T(2,128)(2,1)S(1)} %collective-permute-done), channel_id=1, source_target_pairs={{0,4},{4,8},{8,12},{12,0},{1,5},{5,9},{9,13},{13,1},{2,6},{6,10},{... | collective-permute-start | bytes 196616 | tf_op jit(solution)/shard_map/ppermute | solution.py:73
  24.5 17.1 %copy-start.2 = (pred[640,512]{0,1:T(8,128)(4,1)S(1)}, pred[640,512]{0,1:T(8,128)(4,1)}, u32[]{:S(2)}) copy-start(pred[640,512]{0,1:T(8,128)(4,1)} %fusion.10) | copy-start | bytes 983044
  24.5 17.1 %copy-start.3 = (bf16[128,2,5,128]{3,1,2,0:T(2,128)(2,1)S(1)}, bf16[128,2,5,128]{3,1,2,0:T(2,128)(2,1)}, u32[]{:S(2)}) copy-start(bf16[128,2,5,128]{3,1,2,0:T(2,128)(2,1)} %copy.17) | copy-start | bytes 983044
  26.6 14.4 %collective-permute-start.2 = (bf16[1,128,2,128]{3,2,1,0:T(2,128)(2,1)S(1)}, bf16[1,128,2,128]{3,2,1,0:T(2,128)(2,1)S(1)}, u32[]{:S(2)}, u32[]{:S(2)}) collective-permute-start(bf16[1,128,2,128]{3,2,1,0:T(2,128)(2,1)S(1)} %collective-permute-done.1), channel_id=1, source_target_pairs={{0,4},{4,8},{8,12},{12,0},{1,5},{5,9},{9,13},{13,1},{2,6},{6,10},{... | collective-permute-start | bytes 196616 | tf_op jit(solution)/shard_map/ppermute | solution.py:73
  47.6 46.2 %reduce-scatter.2.cloned.1.call-start = ((), (), s32[]{:S(2)}) async-start(), calls=%async_computation.4 | async-start | bytes 1966080 | tf_op jit(solution)/shard_map/reduce_scatter | solution.py:98
  85.9 13.0 %copy-start.8 = (s32[64]{0:T(128)S(1)}, s32[64]{0:T(128)}, u32[]{:S(2)}) copy-start(s32[64]{0:T(128)} %param.19) | copy-start | bytes 772
  85.9 13.0 %copy-start.5 = (bf16[5120]{0:T(1024)(128)(2,1)S(1)}, bf16[5120]{0:T(1024)(128)(2,1)}, u32[]{:S(2)}) copy-start(bf16[5120]{0:T(1024)(128)(2,1)} %param.16) | copy-start | bytes 30724
  85.9 13.0 %copy-start.6 = (s32[1,64,1]{1,2,0:T(1,128)S(1)}, s32[1,64,1]{1,2,0:T(1,128)}, u32[]{:S(2)}) copy-start(s32[1,64,1]{1,2,0:T(1,128)} %param.18) | copy-start | bytes 772
  93.8 22.7 %all-to-all-start = ((bf16[4,64,1280]{2,1,0:T(8,128)(2,1)}), bf16[4,64,1280]{2,1,0:T(8,128)(2,1)}, u32[]{:S(2)}, u32[]{:S(2)}) async-start(bf16[4,64,1280]{2,1,0:T(8,128)(2,1)} %bitcast.75), calls=%async_computation.1 | async-start | bytes 1310720 | tf_op jit(solution)/shard_map/all_to_all | solution.py:106
  118.6 1.1 copy-start.1
  125.4 19.7 %copy-start.7 = (bf16[5120,32]{0,1:T(8,128)(2,1)S(1)}, bf16[5120,32]{0,1:T(8,128)(2,1)}, u32[]{:S(2)}) copy-start(bf16[5120,32]{0,1:T(8,128)(2,1)} %param.17) | copy-start | bytes 983044
Sparse Core Ops, SparseCore 0:
  47.7 33.8 all-gather.1
  86.0 7.7 reduce-scatter.1
